TPU v7x, 32 devices: a whole 2x2x4 slice. The times are simulated.
32 devices in a mesh: row: 4 (over y, x), col: 8 (over z, core).
Axes of the slice: x: 2, y: 2, z: 4, core: 2. Of those that a mesh axis runs over, the one named last changes fastest.
Arguments:
- loads: float32 [4, 8, 1024, 8], P('row', 'col'), may hold values from -6 to 6
- schur: float32 [4, 8, 1024, 1024], P('row', 'col'), may hold values from -0.5 to 4.5, as said below
- factor: float32 [4, 8, 1024, 1024], P('row', 'col'), may hold values from -0.5 to 0.6, as said below
- coarse_inverse: float32 [1536, 1536], P(('row', 'col')), may hold values from -0.5 to 1.5, as said below
- elements: int32 [4, 8], P('row', 'col'), may hold values from 4096 to 16383
- west_map: int32 [4, 8, 256], P('row', 'col'), may hold values from 0 to 255, each once within a row
- south_map: int32 [4, 8, 256], P('row', 'col'), may hold values from 0 to 255, each once within a row
- prim_local: int32 [4, 8, 48], P('row', 'col'), may hold values from 0 to 1023
- prim_coarse: int32 [4, 8, 48], P('row', 'col'), may hold values from 0 to 1535
Outputs:
- solution: float32 [4, 8, 1024, 8], P('row', 'col')
- residual: float32 [4, 8, 1024, 8], P('row', 'col')
Inputs may be any that keep to these rules, and one draw needn't show every extreme that they name: `schur`: symmetric positive definite. `factor`: symmetric positive definite. `coarse_inverse`: symmetric positive definite. `west_map`: each subdomain's row is a permutation of 0 to 255. `south_map`: each subdomain's row is a permutation of 0 to 255. `prim_local`: values may repeat. `prim_coarse`: values may repeat, within a subdomain and between subdomains.
All inputs are finite; a program needn't handle non-finite values.
Results may differ from a plain program's by a relative error of at most 0.0001.
Values sent between devices are 32-bit elements; how exact they have to be, the bound alone decides.
A program may use at most 128 MiB of HBM per device.

v0:
```python
import jax
import jax.numpy as jnp
from jax import lax
from jax.sharding import PartitionSpec as P

ELEM_BASE = 4096
HIGHEST_PRECISION = lax.Precision.HIGHEST


def from_behind(x, axis, by):
    devices = lax.axis_size(axis)
    pairs = [(i, i + by) for i in range(devices) if 0 <= i + by < devices]
    return lax.ppermute(x, axis, pairs)


def product(matrix, vectors):
    return jnp.dot(matrix, vectors, precision=HIGHEST_PRECISION, preferred_element_type=jnp.float32)


def body(
    loads, schur, factor, coarse_inverse, elements, west_map, south_map, prim_local, prim_coarse
):
    schur_block = schur[0, 0]
    factor_block = factor[0, 0]
    local_loads = loads[0, 0]
    sweep_count = elements[0, 0] // ELEM_BASE
    west_order = west_map[0, 0]
    south_order = south_map[0, 0]
    primal_local = prim_local[0, 0]
    primal_coarse = prim_coarse[0, 0]
    unknowns = schur_block.shape[0]
    face_size = unknowns // 4
    column = lax.axis_index("col")
    grid_row = lax.axis_index("row")
    neighbour_flags = jnp.stack(
        [
            column > 0,
            column < lax.axis_size("col") - 1,
            grid_row > 0,
            grid_row < lax.axis_size("row") - 1,
        ]
    )
    weights = jnp.where(neighbour_flags[jnp.arange(unknowns) // face_size], 0.5, 1.0).astype(
        jnp.float32
    )[:, None]

    def assemble(values):
        west_face = values[:face_size]
        east_face = values[face_size : 2 * face_size]
        south_face = values[2 * face_size : 3 * face_size]
        north_face = values[3 * face_size :]
        from_west = from_behind(east_face, "col", 1)
        west_add = jnp.take(from_west, west_order, axis=0)
        west_back = jnp.zeros_like(west_face).at[west_order].set(west_face)
        from_east = from_behind(west_back, "col", -1)
        from_south = from_behind(north_face, "row", 1)
        south_add = jnp.take(from_south, south_order, axis=0)
        south_back = jnp.zeros_like(south_face).at[south_order].set(south_face)
        from_north = from_behind(south_back, "row", -1)
        return values + jnp.concatenate([west_add, from_east, south_add, from_north], axis=0)

    def weighted_sum(first, second):
        return jnp.sum(weights * first * second, axis=0)

    all_primal = lax.all_gather(primal_coarse, ("row", "col"), axis=0, tiled=True)
    right_side = assemble(local_loads)
    residual = right_side
    scaled = weights * residual
    local = product(factor_block, scaled)

    def sweep(turn, present):
        return present + product(factor_block, scaled - product(schur_block, present))

    local = lax.fori_loop(1, sweep_count, sweep, local)
    picked = jnp.take(scaled, primal_local, axis=0)
    columns = jnp.take(coarse_inverse, all_primal, axis=1)
    solved = product(columns, lax.all_gather(picked, ("row", "col"), axis=0, tiled=True))
    whole = lax.all_gather(solved, ("row", "col"), axis=0, tiled=True)
    precond = assemble(
        weights
        * (
            local
            + jnp.zeros_like(scaled).at[primal_local].add(jnp.take(whole, primal_coarse, axis=0))
        )
    )
    product_now = lax.psum(weighted_sum(residual, precond), ("row", "col"))
    image = assemble(product(schur_block, precond))
    alpha = product_now / lax.psum(weighted_sum(precond, image), ("row", "col"))
    solution = alpha * precond
    residual = residual - alpha * image
    return (solution[None, None], residual[None, None])


def solution(mesh):
    placed = (
        P("row", "col", None, None),
        P("row", "col", None, None),
        P("row", "col", None, None),
        P(("row", "col"), None),
        P("row", "col"),
        P("row", "col", None),
        P("row", "col", None),
        P("row", "col", None),
        P("row", "col", None),
    )
    return jax.shard_map(
        body,
        mesh=mesh,
        in_specs=placed,
        out_specs=(P("row", "col", None, None), P("row", "col", None, None)),
        check_vma=False,
    )
```

profile of v0, /device:TPU:0, one launch (start us, length us, event | category | flops | bytes accessed | tf_op | source)
XLA Modules:
  0.0 256.3 jit_solution(8718719181798448319)
XLA Ops:
  0.6 0.7 compare_select_fusion.3
  1.3 0.7 fusion.39
  2.2 1.2 scatter_custom_fusion
  3.5 1.3 collective-permute-start.1
  4.8 0.7 compare_select_fusion.2
  5.6 1.2 scatter_custom_fusion.1
  6.8 1.3 collective-permute-start.3
  8.3 5.5 %collective-permute-start.2 = (f32[256,8]{1,0:T(8,128)S(1)}, f32[256,8]{1,0:T(8,128)S(1)}, u32[]{:S(2)}, u32[]{:S(2)}) collective-permute-start(f32[256,8]{1,0:T(8,128)S(1)} %bitcast.105), channel_id=1, source_target_pairs={{0,8},{8,16},{16,24},{1,9},{9,17},{17,25},{2,10},{10,18},{18,26},{... | collective-permute-start | bytes 24584 | tf_op jit(solution)/shard_map/ppermute | solution.py:13
  13.9 2.8 %collective-permute-start = (f32[256,8]{1,0:T(8,128)S(1)}, f32[256,8]{1,0:T(8,128)S(1)}, u32[]{:S(2)}, u32[]{:S(2)}) collective-permute-start(f32[256,8]{1,0:T(8,128)S(1)} %bitcast.104), channel_id=1, source_target_pairs={{0,1},{1,2},{2,3},{3,4},{4,5},{5,6},{6,7},{8,9},{9,10},{10,11},{11... | collective-permute-start | bytes 24584 | tf_op jit(solution)/shard_map/ppermute | solution.py:13
  19.3 0.7 compare_and_fusion.2
  20.0 0.7 compare_select_fusion.5
  20.7 0.7 compare_and_fusion.1
  21.4 0.7 compare_select_fusion.4
  22.1 0.7 bitcast_dynamic-update-slice_fusion
  22.8 41.8 %all-reduce = s32[1536]{0:T(1024)S(1)} all-reduce(s32[1536]{0:T(1024)S(1)} %bitcast_dynamic-update-slice_fusion), channel_id=2, replica_groups=mesh['row'=4,'col'=8] {'row','col'}, use_global_device_ids=true, to_apply=%add | all-reduce | flops 1536 | bytes 12288 | tf_op jit(solution)/shard_map/all_gather | solution.py:65
  65.4 1.2 copy.96
  66.6 2.6 %gather_fusion = f32[1536,48]{1,0:T(8,128)S(1)} fusion(f32[48,1536]{0,1:T(8,128)S(1)} %copy.96, s32[2048]{0:T(1024)S(1)} %pad_clamp_fusion), kind=kCustom, calls=%fused_computation.6 | custom fusion | bytes 595968 | tf_op jit(solution)/shard_map/jit(_take)/gather | solution.py:76
  69.2 0.7 gather_fusion.3
  70.0 0.7 gather_fusion.2
  71.1 5.7 %convolution_bitcast_fusion.2 = f32[1024,8]{0,1:T(8,128)S(1)} fusion(f32[1,1,1024,8]{2,3,1,0:T(8,128)S(1)} %copy-done.1, f32[1,1,256,8]{2,3,1,0:T(8,128)S(1)} %bitcast.107, f32[1,1,256,8]{2,3,1,0:T(8,128)S(1)} %bitcast.102, f32[1,1,256,8]{2,3,1,0:T(8,128)S(1)} %bitcast.106, f32[1,1,256,8]{2,3,1,0:T(8,128)S(1)} %bitcast.103, f32[1024]{0:T(1024)S(1)} %bitcast.98, ...), kind=kOutput, calls=%fused_computation.20 | convolution fusion | flops 100704256 | bytes 4296704 | tf_op jit(solution)/shard_map/dot_general | solution.py:17
  76.8 19.1 %while.10 = (s32[]{:T(128)}, f32[1024,8]{0,1:T(8,128)S(1)}, s32[]{:T(128)}, f32[1024,1024]{1,0:T(8,128)}, f32[1024,8]{0,1:T(8,128)S(1)}, /*index=5*/f32[1024,1024]{1,0:T(8,128)}, s32[]{:T(128)}) while((s32[]{:T(128)}, f32[1024,8]{0,1:T(8,128)S(1)}, s32[]{:T(128)}, f32[1024,1024]{1,0:T(8,128)}, f32[1024,8]{0,1:T(8,128)S(1)}, ...), condition=%wide.region_3.5_spmd, body=%wide.region_2.4_spmd.sunk | while | flops 201342976 | bytes 25362536 | solution.py:74
  76.9 5.9 %convolution_subtract_fusion.2 = f32[1024,8]{0,1:T(8,128)S(1)} fusion(f32[1024,8]{0,1:T(8,128)S(1)} %get-tuple-element.125, f32[1024,1024]{1,0:T(8,128)} %get-tuple-element.124, f32[1024,8]{0,1:T(8,128)S(1)} %get-tuple-element.115), kind=kOutput, calls=%fused_computation.18.clone.1 | convolution fusion | flops 100671488 | bytes 4292608 | tf_op jit(solution)/shard_map/while/body/dot_general | solution.py:17
  82.8 3.6 %fusion.55 = f32[1024,8]{0,1:T(8,128)S(1)} fusion(f32[1024,8]{0,1:T(8,128)S(1)} %get-tuple-element.115, f32[1024,8]{0,1:T(8,128)S(1)} %convolution_subtract_fusion.2, f32[1024,1024]{1,0:T(8,128)S(1)} %copy-done), kind=kOutput, calls=%fused_computation.17.clone.1 | convolution fusion | flops 100671488 | bytes 4292608 | tf_op jit(solution)/shard_map/while/body/dot_general | solution.py:17
  86.4 5.9 %convolution_subtract_fusion.2 = f32[1024,8]{0,1:T(8,128)S(1)} fusion(f32[1024,8]{0,1:T(8,128)S(1)} %get-tuple-element.125, f32[1024,1024]{1,0:T(8,128)} %get-tuple-element.124, f32[1024,8]{0,1:T(8,128)S(1)} %get-tuple-element.115), kind=kOutput, calls=%fused_computation.18.clone.1 | convolution fusion | flops 100671488 | bytes 4292608 | tf_op jit(solution)/shard_map/while/body/dot_general | solution.py:17
  92.3 3.6 %fusion.55 = f32[1024,8]{0,1:T(8,128)S(1)} fusion(f32[1024,8]{0,1:T(8,128)S(1)} %get-tuple-element.115, f32[1024,8]{0,1:T(8,128)S(1)} %convolution_subtract_fusion.2, f32[1024,1024]{1,0:T(8,128)S(1)} %copy-done), kind=kOutput, calls=%fused_computation.17.clone.1 | convolution fusion | flops 100671488 | bytes 4292608 | tf_op jit(solution)/shard_map/while/body/dot_general | solution.py:17
  96.8 37.1 %all-gather.1 = f32[32,48,8]{1,2,0:T(8,128)S(1)} all-gather(f32[1,48,8]{1,2,0:T(8,128)S(1)} %copy.98), channel_id=1, replica_groups=mesh['row'=4,'col'=8] {'row','col'}, dimensions={0}, use_global_device_ids=true | all-gather | bytes 50688 | tf_op jit(solution)/shard_map/all_gather | solution.py:77
  134.7 38.6 %all-gather.2 = f32[32,48,8]{1,2,0:T(8,128)S(1)} all-gather(f32[1,48,8]{1,2,0:T(8,128)S(1)} %convolution_bitcast_fusion.3), channel_id=1, replica_groups=mesh['row'=4,'col'=8] {'row','col'}, dimensions={0}, use_global_device_ids=true | all-gather | bytes 50688 | tf_op jit(solution)/shard_map/all_gather | solution.py:78
  173.5 1.1 scatter_custom_fusion.2
  174.9 1.3 collective-permute-start.6
  176.1 2.2 collective-permute-start.4
  178.5 1.2 scatter_custom_fusion.4
  179.8 1.3 collective-permute-start.7
  181.2 1.2 scatter_custom_fusion.3
  182.5 1.5 collective-permute-start.5
  184.1 0.7 gather_fusion.5
  185.1 0.7 gather_fusion.4
  185.9 3.0 %collective-permute-done.7 = f32[256,8]{0,1:T(8,128)S(1)} collective-permute-done((f32[256,8]{0,1:T(8,128)S(1)}, f32[256,8]{0,1:T(8,128)S(1)}, u32[]{:S(2)}, u32[]{:S(2)}) %collective-permute-start.7) | collective-permute-done | bytes 8224 | tf_op jit(solution)/shard_map/ppermute | solution.py:13
  188.9 5.6 %convolution_bitcast_fusion.1 = f32[1024,8]{0,1:T(8,128)S(1)} fusion(f32[1024,8]{0,1:T(8,128)S(1)} %maximum_add_fusion.2, f32[1,1,1024,1024]{3,2,1,0:T(8,128)} %bitcast.95), kind=kOutput, calls=%fused_computation.19 | convolution fusion | flops 100663296 | bytes 4259840 | tf_op jit(solution)/shard_map/dot_general | solution.py:17
  194.6 5.9 %collective-permute-start.10 = (f32[256,8]{0,1:T(8,128)S(1)}, f32[256,8]{0,1:T(8,128)S(1)}, u32[]{:S(2)}, u32[]{:S(2)}) collective-permute-start(f32[256,8]{0,1:T(8,128)S(1)} %get-tuple-element.55), channel_id=1, source_target_pairs={{0,8},{8,16},{16,24},{1,9},{9,17},{17,25},{2,10},{10,18},{18,26},{... | collective-permute-start | bytes 24584 | tf_op jit(solution)/shard_map/ppermute | solution.py:13
  200.6 4.0 %collective-permute-start.8 = (f32[256,8]{0,1:T(8,128)S(1)}, f32[256,8]{0,1:T(8,128)S(1)}, u32[]{:S(2)}, u32[]{:S(2)}) collective-permute-start(f32[256,8]{0,1:T(8,128)S(1)} %get-tuple-element.53), channel_id=1, source_target_pairs={{0,1},{1,2},{2,3},{3,4},{4,5},{5,6},{6,7},{8,9},{9,10},{10,11},{11... | collective-permute-start | bytes 24584 | tf_op jit(solution)/shard_map/ppermute | solution.py:13
  204.7 1.2 scatter_custom_fusion.6
  206.0 1.3 collective-permute-start.11
  207.4 1.2 scatter_custom_fusion.5
  208.7 1.3 collective-permute-start.9
  210.1 0.7 gather_fusion.7
  211.0 0.7 gather_fusion.6
  212.5 43.1 %all-reduce.1 = (f32[8]{0:T(128)S(1)}, f32[8]{0:T(128)S(1)}) all-reduce(f32[8]{0:T(128)S(1)} %get-tuple-element.38, f32[8]{0:T(128)S(1)} %get-tuple-element.37), channel_id=1, replica_groups=mesh['row'=4,'col'=8] {'row','col'}, use_global_device_ids=true, to_apply=%region_8.10 | all-reduce | flops 16 | bytes 128 | tf_op jit(solution)/shard_map/psum | solution.py:86
  255.6 0.7 subtract_bitcast_fusion
  (76 shorter events, 8.0 us)
Async XLA Ops:
  0.6 70.3 %copy-start.1 = (f32[1,1,1024,8]{2,3,1,0:T(8,128)S(1)}, f32[1,1,1024,8]{2,3,1,0:T(8,128)}, u32[]{:S(2)}) copy-start(f32[1,1,1024,8]{2,3,1,0:T(8,128)} %param.13) | copy-start | bytes 98308
  3.5 67.4 %collective-permute-start.1 = (f32[256,8]{0,1:T(8,128)S(1)}, f32[256,8]{0,1:T(8,128)S(1)}, u32[]{:S(2)}, u32[]{:S(2)}) collective-permute-start(f32[256,8]{0,1:T(8,128)S(1)} %copy.91), channel_id=1, source_target_pairs={{1,0},{2,1},{3,2},{4,3},{5,4},{6,5},{7,6},{9,8},{10,9},{11,10},{12... | collective-permute-start | bytes 24584 | tf_op jit(solution)/shard_map/ppermute | solution.py:13
  6.8 64.0 %collective-permute-start.3 = (f32[256,8]{0,1:T(8,128)S(1)}, f32[256,8]{0,1:T(8,128)S(1)}, u32[]{:S(2)}, u32[]{:S(2)}) collective-permute-start(f32[256,8]{0,1:T(8,128)S(1)} %copy.95), channel_id=1, source_target_pairs={{8,0},{16,8},{24,16},{9,1},{17,9},{25,17},{10,2},{18,10},{26,18},{... | collective-permute-start | bytes 24584 | tf_op jit(solution)/shard_map/ppermute | solution.py:13
  8.3 61.0 %collective-permute-start.2 = (f32[256,8]{1,0:T(8,128)S(1)}, f32[256,8]{1,0:T(8,128)S(1)}, u32[]{:S(2)}, u32[]{:S(2)}) collective-permute-start(f32[256,8]{1,0:T(8,128)S(1)} %bitcast.105), channel_id=1, source_target_pairs={{0,8},{8,16},{16,24},{1,9},{9,17},{17,25},{2,10},{10,18},{18,26},{... | collective-permute-start | bytes 24584 | tf_op jit(solution)/shard_map/ppermute | solution.py:13
  13.9 56.1 %collective-permute-start = (f32[256,8]{1,0:T(8,128)S(1)}, f32[256,8]{1,0:T(8,128)S(1)}, u32[]{:S(2)}, u32[]{:S(2)}) collective-permute-start(f32[256,8]{1,0:T(8,128)S(1)} %bitcast.104), channel_id=1, source_target_pairs={{0,1},{1,2},{2,3},{3,4},{4,5},{5,6},{6,7},{8,9},{9,10},{10,11},{11... | collective-permute-start | bytes 24584 | tf_op jit(solution)/shard_map/ppermute | solution.py:13
  76.9 5.9 %copy-start = (f32[1024,1024]{1,0:T(8,128)S(1)}, f32[1024,1024]{1,0:T(8,128)}, u32[]{:S(2)}) copy-start(f32[1024,1024]{1,0:T(8,128)} %get-tuple-element.126) | copy-start | bytes 12582916 | tf_op jit(solution)/shard_map/while
  86.4 5.9 %copy-start = (f32[1024,1024]{1,0:T(8,128)S(1)}, f32[1024,1024]{1,0:T(8,128)}, u32[]{:S(2)}) copy-start(f32[1024,1024]{1,0:T(8,128)} %get-tuple-element.126) | copy-start | bytes 12582916 | tf_op jit(solution)/shard_map/while
  174.9 9.1 %collective-permute-start.6 = (f32[256,8]{0,1:T(8,128)S(1)}, f32[256,8]{0,1:T(8,128)S(1)}, u32[]{:S(2)}, u32[]{:S(2)}) collective-permute-start(f32[256,8]{0,1:T(8,128)S(1)} %get-tuple-element.59), channel_id=1, source_target_pairs={{0,8},{8,16},{16,24},{1,9},{9,17},{17,25},{2,10},{10,18},{18,26},{... | collective-permute-start | bytes 24584 | tf_op jit(solution)/shard_map/ppermute | solution.py:13
  176.1 8.8 %collective-permute-start.4 = (f32[256,8]{0,1:T(8,128)S(1)}, f32[256,8]{0,1:T(8,128)S(1)}, u32[]{:S(2)}, u32[]{:S(2)}) collective-permute-start(f32[256,8]{0,1:T(8,128)S(1)} %get-tuple-element.57), channel_id=1, source_target_pairs={{0,1},{1,2},{2,3},{3,4},{4,5},{5,6},{6,7},{8,9},{9,10},{10,11},{11... | collective-permute-start | bytes 24584 | tf_op jit(solution)/shard_map/ppermute | solution.py:13
  179.8 9.1 %collective-permute-start.7 = (f32[256,8]{0,1:T(8,128)S(1)}, f32[256,8]{0,1:T(8,128)S(1)}, u32[]{:S(2)}, u32[]{:S(2)}) collective-permute-start(f32[256,8]{0,1:T(8,128)S(1)} %copy.111), channel_id=1, source_target_pairs={{8,0},{16,8},{24,16},{9,1},{17,9},{25,17},{10,2},{18,10},{26,18},{... | collective-permute-start | bytes 24584 | tf_op jit(solution)/shard_map/ppermute | solution.py:13
  182.5 6.4 %collective-permute-start.5 = (f32[256,8]{0,1:T(8,128)S(1)}, f32[256,8]{0,1:T(8,128)S(1)}, u32[]{:S(2)}, u32[]{:S(2)}) collective-permute-start(f32[256,8]{0,1:T(8,128)S(1)} %copy.107), channel_id=1, source_target_pairs={{1,0},{2,1},{3,2},{4,3},{5,4},{6,5},{7,6},{9,8},{10,9},{11,10},{12... | collective-permute-start | bytes 24584 | tf_op jit(solution)/shard_map/ppermute | solution.py:13
  194.6 15.4 %collective-permute-start.10 = (f32[256,8]{0,1:T(8,128)S(1)}, f32[256,8]{0,1:T(8,128)S(1)}, u32[]{:S(2)}, u32[]{:S(2)}) collective-permute-start(f32[256,8]{0,1:T(8,128)S(1)} %get-tuple-element.55), channel_id=1, source_target_pairs={{0,8},{8,16},{16,24},{1,9},{9,17},{17,25},{2,10},{10,18},{18,26},{... | collective-permute-start | bytes 24584 | tf_op jit(solution)/shard_map/ppermute | solution.py:13
  200.6 10.4 %collective-permute-start.8 = (f32[256,8]{0,1:T(8,128)S(1)}, f32[256,8]{0,1:T(8,128)S(1)}, u32[]{:S(2)}, u32[]{:S(2)}) collective-permute-start(f32[256,8]{0,1:T(8,128)S(1)} %get-tuple-element.53), channel_id=1, source_target_pairs={{0,1},{1,2},{2,3},{3,4},{4,5},{5,6},{6,7},{8,9},{9,10},{10,11},{11... | collective-permute-start | bytes 24584 | tf_op jit(solution)/shard_map/ppermute | solution.py:13
  206.0 6.2 %collective-permute-start.11 = (f32[256,8]{0,1:T(8,128)S(1)}, f32[256,8]{0,1:T(8,128)S(1)}, u32[]{:S(2)}, u32[]{:S(2)}) collective-permute-start(f32[256,8]{0,1:T(8,128)S(1)} %copy.119), channel_id=1, source_target_pairs={{8,0},{16,8},{24,16},{9,1},{17,9},{25,17},{10,2},{18,10},{26,18},{... | collective-permute-start | bytes 24584 | tf_op jit(solution)/shard_map/ppermute | solution.py:13
  208.7 3.7 %collective-permute-start.9 = (f32[256,8]{0,1:T(8,128)S(1)}, f32[256,8]{0,1:T(8,128)S(1)}, u32[]{:S(2)}, u32[]{:S(2)}) collective-permute-start(f32[256,8]{0,1:T(8,128)S(1)} %copy.115), channel_id=1, source_target_pairs={{1,0},{2,1},{3,2},{4,3},{5,4},{6,5},{7,6},{9,8},{10,9},{11,10},{12... | collective-permute-start | bytes 24584 | tf_op jit(solution)/shard_map/ppermute | solution.py:13
where the time goes:
time: 257 us; the launch traced here: 256 us
  blocking collectives  161 us (63%)
  matrix products  30.9 us (12%)
  starting transfers between devices  29.8 us (12%)
  local copies, waits for them, and re-layouts  20.7 us (8%)
  other arithmetic  8.95 us (3%)
  waiting for transfers between devices  3.55 us (1%)
    psum x1, blocking collectives, body(): product_now = lax.psum(weighted_sum(residual, precond), ('row', 'col'))  43.1 us
    all_gather x1, blocking collectives, body(): lax.all_gather(primal_coarse, ('row', 'col'), axis=0, tiled=True)  41.8 us
    all_gather x1, blocking collectives, body(): whole = lax.all_gather(solved, ('row', 'col'), axis=0, tiled=True)  38.6 us
    all_gather x1, blocking collectives, body(): lax.all_gather(picked, ('row', 'col'), axis=0, tiled=True)  37.1 us
    dot_general x7, matrix products, product(): jnp.dot(matrix, vectors, precision=HIGHEST_PRECISION, preferred_element_t...  30.9 us
    ppermute x12, starting transfers between devices, from_behind(): return lax.ppermute(x, axis, pairs)  29.8 us
  transfers between devices with their start and end apart: 12, of which 3 were waited for; matrix products, arithmetic and copies ran while one was open for 9% of the time, Pallas kernels for 0%

commit v1 on v0

--- a/solution.py
+++ b/solution.py
@@ -83,7 +83,7 @@
             + jnp.zeros_like(scaled).at[primal_local].add(jnp.take(whole, primal_coarse, axis=0))
         )
     )
-    product_now = lax.psum(weighted_sum(residual, precond), ("row", "col"))
+    product_now = lax.psum(lax.psum(weighted_sum(residual, precond), "col"), "row")
     image = assemble(product(schur_block, precond))
     alpha = product_now / lax.psum(weighted_sum(precond, image), ("row", "col"))
     solution = alpha * precond

time: 257 us -> 281 us (1.093)
  blocking collectives: 161 us -> 184 us
    psum x1 -> x3, blocking collectives: 43.1 us -> 66.4 us  [the longest x1 39.3 us: body(): alpha = product_now / lax.psum(weighted_sum(precond, image), ('row', 'col'))]
  transfers between devices with their start and end apart: 12 -> 12, of which waited for: 3 -> 3; matrix products, arithmetic and copies ran while one was open for 9% -> 8% of each run, Pallas kernels for 0% -> 0%
where the time goes in v1:
time: 281 us; the launch traced here: 280 us
  blocking collectives  184 us (65%)
  matrix products  30.9 us (11%)
  starting transfers between devices  29.8 us (11%)
  local copies, waits for them, and re-layouts  20.7 us (7%)
  other arithmetic  8.95 us (3%)
  waiting for transfers between devices  3.55 us (1%)
    all_gather x1, blocking collectives, body(): lax.all_gather(primal_coarse, ('row', 'col'), axis=0, tiled=True)  41.8 us
    psum x1, blocking collectives, body(): alpha = product_now / lax.psum(weighted_sum(precond, image), ('row', 'col'))  39.3 us
    all_gather x1, blocking collectives, body(): whole = lax.all_gather(solved, ('row', 'col'), axis=0, tiled=True)  38.6 us
    all_gather x1, blocking collectives, body(): lax.all_gather(picked, ('row', 'col'), axis=0, tiled=True)  37.1 us
    dot_general x7, matrix products, product(): jnp.dot(matrix, vectors, precision=HIGHEST_PRECISION, preferred_element_t...  30.9 us
    ppermute x12, starting transfers between devices, from_behind(): return lax.ppermute(x, axis, pairs)  29.8 us
    psum x1, blocking collectives, body(): lax.psum(weighted_sum(residual, precond), 'col')  16 us
    psum x1, blocking collectives, body(): lax.psum(lax.psum(weighted_sum(residual, precond), 'col'), 'row')  11.2 us
  transfers between devices with their start and end apart: 12, of which 3 were waited for; matrix products, arithmetic and copies ran while one was open for 8% of the time, Pallas kernels for 0%

profile of v1, /device:TPU:0, one launch (start us, length us, event | category | flops | bytes accessed | tf_op | source)
XLA Modules:
  0.0 279.6 jit_solution(6947299285947438443)
XLA Ops:
  0.6 0.7 compare_select_fusion.3
  1.3 0.7 fusion.39
  2.2 1.2 scatter_custom_fusion
  3.5 1.3 collective-permute-start.1
  4.8 0.7 compare_select_fusion.2
  5.6 1.2 scatter_custom_fusion.1
  6.8 1.3 collective-permute-start.3
  8.3 5.5 %collective-permute-start.2 = (f32[256,8]{1,0:T(8,128)S(1)}, f32[256,8]{1,0:T(8,128)S(1)}, u32[]{:S(2)}, u32[]{:S(2)}) collective-permute-start(f32[256,8]{1,0:T(8,128)S(1)} %bitcast.105), channel_id=1, source_target_pairs={{0,8},{8,16},{16,24},{1,9},{9,17},{17,25},{2,10},{10,18},{18,26},{... | collective-permute-start | bytes 24584 | tf_op jit(solution)/shard_map/ppermute | solution.py:13
  13.9 2.8 collective-permute-start
  19.3 0.7 compare_and_fusion.2
  20.7 0.7 compare_and_fusion.1
  22.1 0.7 bitcast_dynamic-update-slice_fusion
  22.8 41.8 %all-reduce = s32[1536]{0:T(1024)S(1)} all-reduce(s32[1536]{0:T(1024)S(1)} %bitcast_dynamic-update-slice_fusion), channel_id=2, replica_groups=mesh['row'=4,'col'=8] {'row','col'}, use_global_device_ids=true, to_apply=%add | all-reduce | flops 1536 | bytes 12288 | tf_op jit(solution)/shard_map/all_gather | solution.py:65
  65.4 1.2 copy.96
  66.6 2.6 gather_fusion
  69.2 0.7 gather_fusion.3
  70.0 0.7 gather_fusion.2
  71.1 5.7 %convolution_bitcast_fusion.2 = f32[1024,8]{0,1:T(8,128)S(1)} fusion(f32[1,1,1024,8]{2,3,1,0:T(8,128)S(1)} %copy-done.1, f32[1,1,256,8]{2,3,1,0:T(8,128)S(1)} %bitcast.107, f32[1,1,256,8]{2,3,1,0:T(8,128)S(1)} %bitcast.102, f32[1,1,256,8]{2,3,1,0:T(8,128)S(1)} %bitcast.106, f32[1,1,256,8]{2,3,1,0:T(8,128)S(1)} %bitcast.103, f32[1024]{0:T(1024)S(1)} %bitcast.98, ...), kind=kOutput, calls=%fused_computation.20 | convolution fusion | flops 100704256 | bytes 4296704 | tf_op jit(solution)/shard_map/dot_general | solution.py:17
  76.8 19.1 %while.10 = (s32[]{:T(128)}, f32[1024,8]{0,1:T(8,128)S(1)}, s32[]{:T(128)}, f32[1024,1024]{1,0:T(8,128)}, f32[1024,8]{0,1:T(8,128)S(1)}, /*index=5*/f32[1024,1024]{1,0:T(8,128)}, s32[]{:T(128)}) while((s32[]{:T(128)}, f32[1024,8]{0,1:T(8,128)S(1)}, s32[]{:T(128)}, f32[1024,1024]{1,0:T(8,128)}, f32[1024,8]{0,1:T(8,128)S(1)}, ...), condition=%wide.region_3.5_spmd, body=%wide.region_2.4_spmd.sunk | while | flops 201342976 | bytes 25362536 | solution.py:74
  76.9 5.9 %convolution_subtract_fusion.2 = f32[1024,8]{0,1:T(8,128)S(1)} fusion(f32[1024,8]{0,1:T(8,128)S(1)} %get-tuple-element.123, f32[1024,1024]{1,0:T(8,128)} %get-tuple-element.122, f32[1024,8]{0,1:T(8,128)S(1)} %get-tuple-element.113), kind=kOutput, calls=%fused_computation.18.clone.1 | convolution fusion | flops 100671488 | bytes 4292608 | tf_op jit(solution)/shard_map/while/body/dot_general | solution.py:17
  82.8 3.6 %fusion.55 = f32[1024,8]{0,1:T(8,128)S(1)} fusion(f32[1024,8]{0,1:T(8,128)S(1)} %get-tuple-element.113, f32[1024,8]{0,1:T(8,128)S(1)} %convolution_subtract_fusion.2, f32[1024,1024]{1,0:T(8,128)S(1)} %copy-done), kind=kOutput, calls=%fused_computation.17.clone.1 | convolution fusion | flops 100671488 | bytes 4292608 | tf_op jit(solution)/shard_map/while/body/dot_general | solution.py:17
  86.4 5.9 %convolution_subtract_fusion.2 = f32[1024,8]{0,1:T(8,128)S(1)} fusion(f32[1024,8]{0,1:T(8,128)S(1)} %get-tuple-element.123, f32[1024,1024]{1,0:T(8,128)} %get-tuple-element.122, f32[1024,8]{0,1:T(8,128)S(1)} %get-tuple-element.113), kind=kOutput, calls=%fused_computation.18.clone.1 | convolution fusion | flops 100671488 | bytes 4292608 | tf_op jit(solution)/shard_map/while/body/dot_general | solution.py:17
  92.3 3.6 %fusion.55 = f32[1024,8]{0,1:T(8,128)S(1)} fusion(f32[1024,8]{0,1:T(8,128)S(1)} %get-tuple-element.113, f32[1024,8]{0,1:T(8,128)S(1)} %convolution_subtract_fusion.2, f32[1024,1024]{1,0:T(8,128)S(1)} %copy-done), kind=kOutput, calls=%fused_computation.17.clone.1 | convolution fusion | flops 100671488 | bytes 4292608 | tf_op jit(solution)/shard_map/while/body/dot_general | solution.py:17
  96.8 37.1 %all-gather.1 = f32[32,48,8]{1,2,0:T(8,128)S(1)} all-gather(f32[1,48,8]{1,2,0:T(8,128)S(1)} %copy.98), channel_id=1, replica_groups=mesh['row'=4,'col'=8] {'row','col'}, dimensions={0}, use_global_device_ids=true | all-gather | bytes 50688 | tf_op jit(solution)/shard_map/all_gather | solution.py:77
  134.7 38.6 %all-gather.2 = f32[32,48,8]{1,2,0:T(8,128)S(1)} all-gather(f32[1,48,8]{1,2,0:T(8,128)S(1)} %convolution_bitcast_fusion.3), channel_id=1, replica_groups=mesh['row'=4,'col'=8] {'row','col'}, dimensions={0}, use_global_device_ids=true | all-gather | bytes 50688 | tf_op jit(solution)/shard_map/all_gather | solution.py:78
  173.5 1.1 scatter_custom_fusion.2
  174.9 1.3 collective-permute-start.6
  176.1 2.2 collective-permute-start.4
  178.5 1.2 scatter_custom_fusion.4
  179.8 1.3 collective-permute-start.7
  181.2 1.2 scatter_custom_fusion.3
  182.5 1.5 collective-permute-start.5
  184.1 0.7 gather_fusion.5
  185.1 0.7 gather_fusion.4
  185.9 3.0 %collective-permute-done.7 = f32[256,8]{0,1:T(8,128)S(1)} collective-permute-done((f32[256,8]{0,1:T(8,128)S(1)}, f32[256,8]{0,1:T(8,128)S(1)}, u32[]{:S(2)}, u32[]{:S(2)}) %collective-permute-start.7) | collective-permute-done | bytes 8224 | tf_op jit(solution)/shard_map/ppermute | solution.py:13
  188.9 5.6 %convolution_bitcast_fusion.1 = f32[1024,8]{0,1:T(8,128)S(1)} fusion(f32[1024,8]{0,1:T(8,128)S(1)} %maximum_add_fusion.2, f32[1,1,1024,1024]{3,2,1,0:T(8,128)} %bitcast.95), kind=kOutput, calls=%fused_computation.19 | convolution fusion | flops 100663296 | bytes 4259840 | tf_op jit(solution)/shard_map/dot_general | solution.py:17
  194.6 5.9 %collective-permute-start.10 = (f32[256,8]{0,1:T(8,128)S(1)}, f32[256,8]{0,1:T(8,128)S(1)}, u32[]{:S(2)}, u32[]{:S(2)}) collective-permute-start(f32[256,8]{0,1:T(8,128)S(1)} %get-tuple-element.53), channel_id=1, source_target_pairs={{0,8},{8,16},{16,24},{1,9},{9,17},{17,25},{2,10},{10,18},{18,26},{... | collective-permute-start | bytes 24584 | tf_op jit(solution)/shard_map/ppermute | solution.py:13
  200.6 4.0 %collective-permute-start.8 = (f32[256,8]{0,1:T(8,128)S(1)}, f32[256,8]{0,1:T(8,128)S(1)}, u32[]{:S(2)}, u32[]{:S(2)}) collective-permute-start(f32[256,8]{0,1:T(8,128)S(1)} %get-tuple-element.51), channel_id=1, source_target_pairs={{0,1},{1,2},{2,3},{3,4},{4,5},{5,6},{6,7},{8,9},{9,10},{10,11},{11... | collective-permute-start | bytes 24584 | tf_op jit(solution)/shard_map/ppermute | solution.py:13
  204.7 1.2 scatter_custom_fusion.6
  206.0 1.3 collective-permute-start.11
  207.4 1.2 scatter_custom_fusion.5
  208.7 1.3 collective-permute-start.9
  210.1 0.7 gather_fusion.7
  211.0 0.7 gather_fusion.6
  212.5 16.0 %psum.21 = f32[8]{0:T(128)S(1)} all-reduce(f32[8]{0:T(128)S(1)} %get-tuple-element.38), channel_id=1, replica_groups=mesh['row'=4,'col'=8] {'col'}, use_global_device_ids=true, to_apply=%region_8.10 | all-reduce | flops 8 | bytes 64 | tf_op jit(solution)/shard_map/psum | solution.py:86
  228.5 39.3 %psum.23 = f32[8]{0:T(128)S(1)} all-reduce(f32[8]{0:T(128)S(1)} %get-tuple-element.37), channel_id=1, replica_groups=mesh['row'=4,'col'=8] {'row','col'}, use_global_device_ids=true, to_apply=%region_13.15 | all-reduce | flops 8 | bytes 64 | tf_op jit(solution)/shard_map/psum | solution.py:88
  267.8 11.2 %psum.22 = f32[8]{0:T(128)S(1)} all-reduce(f32[8]{0:T(128)S(1)} %psum.21), channel_id=1, replica_groups=mesh['row'=4,'col'=8] {'row'}, use_global_device_ids=true, to_apply=%region_9.11 | all-reduce | flops 8 | bytes 64 | tf_op jit(solution)/shard_map/psum | solution.py:86
  278.9 0.7 subtract_bitcast_fusion
  (78 shorter events, 9.3 us)
Async XLA Ops:
  0.6 70.3 %copy-start.1 = (f32[1,1,1024,8]{2,3,1,0:T(8,128)S(1)}, f32[1,1,1024,8]{2,3,1,0:T(8,128)}, u32[]{:S(2)}) copy-start(f32[1,1,1024,8]{2,3,1,0:T(8,128)} %param.13) | copy-start | bytes 98308
  3.5 67.4 %collective-permute-start.1 = (f32[256,8]{0,1:T(8,128)S(1)}, f32[256,8]{0,1:T(8,128)S(1)}, u32[]{:S(2)}, u32[]{:S(2)}) collective-permute-start(f32[256,8]{0,1:T(8,128)S(1)} %copy.91), channel_id=1, source_target_pairs={{1,0},{2,1},{3,2},{4,3},{5,4},{6,5},{7,6},{9,8},{10,9},{11,10},{12... | collective-permute-start | bytes 24584 | tf_op jit(solution)/shard_map/ppermute | solution.py:13
  6.8 64.0 %collective-permute-start.3 = (f32[256,8]{0,1:T(8,128)S(1)}, f32[256,8]{0,1:T(8,128)S(1)}, u32[]{:S(2)}, u32[]{:S(2)}) collective-permute-start(f32[256,8]{0,1:T(8,128)S(1)} %copy.95), channel_id=1, source_target_pairs={{8,0},{16,8},{24,16},{9,1},{17,9},{25,17},{10,2},{18,10},{26,18},{... | collective-permute-start | bytes 24584 | tf_op jit(solution)/shard_map/ppermute | solution.py:13
  8.3 61.0 %collective-permute-start.2 = (f32[256,8]{1,0:T(8,128)S(1)}, f32[256,8]{1,0:T(8,128)S(1)}, u32[]{:S(2)}, u32[]{:S(2)}) collective-permute-start(f32[256,8]{1,0:T(8,128)S(1)} %bitcast.105), channel_id=1, source_target_pairs={{0,8},{8,16},{16,24},{1,9},{9,17},{17,25},{2,10},{10,18},{18,26},{... | collective-permute-start | bytes 24584 | tf_op jit(solution)/shard_map/ppermute | solution.py:13
  13.9 56.1 %collective-permute-start = (f32[256,8]{1,0:T(8,128)S(1)}, f32[256,8]{1,0:T(8,128)S(1)}, u32[]{:S(2)}, u32[]{:S(2)}) collective-permute-start(f32[256,8]{1,0:T(8,128)S(1)} %bitcast.104), channel_id=1, source_target_pairs={{0,1},{1,2},{2,3},{3,4},{4,5},{5,6},{6,7},{8,9},{9,10},{10,11},{11... | collective-permute-start | bytes 24584 | tf_op jit(solution)/shard_map/ppermute | solution.py:13
  76.9 5.9 %copy-start = (f32[1024,1024]{1,0:T(8,128)S(1)}, f32[1024,1024]{1,0:T(8,128)}, u32[]{:S(2)}) copy-start(f32[1024,1024]{1,0:T(8,128)} %get-tuple-element.124) | copy-start | bytes 12582916 | tf_op jit(solution)/shard_map/while
  86.4 5.9 %copy-start = (f32[1024,1024]{1,0:T(8,128)S(1)}, f32[1024,1024]{1,0:T(8,128)}, u32[]{:S(2)}) copy-start(f32[1024,1024]{1,0:T(8,128)} %get-tuple-element.124) | copy-start | bytes 12582916 | tf_op jit(solution)/shard_map/while
  174.9 9.1 %collective-permute-start.6 = (f32[256,8]{0,1:T(8,128)S(1)}, f32[256,8]{0,1:T(8,128)S(1)}, u32[]{:S(2)}, u32[]{:S(2)}) collective-permute-start(f32[256,8]{0,1:T(8,128)S(1)} %get-tuple-element.57), channel_id=1, source_target_pairs={{0,8},{8,16},{16,24},{1,9},{9,17},{17,25},{2,10},{10,18},{18,26},{... | collective-permute-start | bytes 24584 | tf_op jit(solution)/shard_map/ppermute | solution.py:13
  176.1 8.8 %collective-permute-start.4 = (f32[256,8]{0,1:T(8,128)S(1)}, f32[256,8]{0,1:T(8,128)S(1)}, u32[]{:S(2)}, u32[]{:S(2)}) collective-permute-start(f32[256,8]{0,1:T(8,128)S(1)} %get-tuple-element.55), channel_id=1, source_target_pairs={{0,1},{1,2},{2,3},{3,4},{4,5},{5,6},{6,7},{8,9},{9,10},{10,11},{11... | collective-permute-start | bytes 24584 | tf_op jit(solution)/shard_map/ppermute | solution.py:13
  179.8 9.1 %collective-permute-start.7 = (f32[256,8]{0,1:T(8,128)S(1)}, f32[256,8]{0,1:T(8,128)S(1)}, u32[]{:S(2)}, u32[]{:S(2)}) collective-permute-start(f32[256,8]{0,1:T(8,128)S(1)} %copy.111), channel_id=1, source_target_pairs={{8,0},{16,8},{24,16},{9,1},{17,9},{25,17},{10,2},{18,10},{26,18},{... | collective-permute-start | bytes 24584 | tf_op jit(solution)/shard_map/ppermute | solution.py:13
  182.5 6.4 %collective-permute-start.5 = (f32[256,8]{0,1:T(8,128)S(1)}, f32[256,8]{0,1:T(8,128)S(1)}, u32[]{:S(2)}, u32[]{:S(2)}) collective-permute-start(f32[256,8]{0,1:T(8,128)S(1)} %copy.107), channel_id=1, source_target_pairs={{1,0},{2,1},{3,2},{4,3},{5,4},{6,5},{7,6},{9,8},{10,9},{11,10},{12... | collective-permute-start | bytes 24584 | tf_op jit(solution)/shard_map/ppermute | solution.py:13
  194.6 15.4 %collective-permute-start.10 = (f32[256,8]{0,1:T(8,128)S(1)}, f32[256,8]{0,1:T(8,128)S(1)}, u32[]{:S(2)}, u32[]{:S(2)}) collective-permute-start(f32[256,8]{0,1:T(8,128)S(1)} %get-tuple-element.53), channel_id=1, source_target_pairs={{0,8},{8,16},{16,24},{1,9},{9,17},{17,25},{2,10},{10,18},{18,26},{... | collective-permute-start | bytes 24584 | tf_op jit(solution)/shard_map/ppermute | solution.py:13
  200.6 10.4 %collective-permute-start.8 = (f32[256,8]{0,1:T(8,128)S(1)}, f32[256,8]{0,1:T(8,128)S(1)}, u32[]{:S(2)}, u32[]{:S(2)}) collective-permute-start(f32[256,8]{0,1:T(8,128)S(1)} %get-tuple-element.51), channel_id=1, source_target_pairs={{0,1},{1,2},{2,3},{3,4},{4,5},{5,6},{6,7},{8,9},{9,10},{10,11},{11... | collective-permute-start | bytes 24584 | tf_op jit(solution)/shard_map/ppermute | solution.py:13
  206.0 6.2 %collective-permute-start.11 = (f32[256,8]{0,1:T(8,128)S(1)}, f32[256,8]{0,1:T(8,128)S(1)}, u32[]{:S(2)}, u32[]{:S(2)}) collective-permute-start(f32[256,8]{0,1:T(8,128)S(1)} %copy.119), channel_id=1, source_target_pairs={{8,0},{16,8},{24,16},{9,1},{17,9},{25,17},{10,2},{18,10},{26,18},{... | collective-permute-start | bytes 24584 | tf_op jit(solution)/shard_map/ppermute | solution.py:13
  208.7 3.7 %collective-permute-start.9 = (f32[256,8]{0,1:T(8,128)S(1)}, f32[256,8]{0,1:T(8,128)S(1)}, u32[]{:S(2)}, u32[]{:S(2)}) collective-permute-start(f32[256,8]{0,1:T(8,128)S(1)} %copy.115), channel_id=1, source_target_pairs={{1,0},{2,1},{3,2},{4,3},{5,4},{6,5},{7,6},{9,8},{10,9},{11,10},{12... | collective-permute-start | bytes 24584 | tf_op jit(solution)/shard_map/ppermute | solution.py:13
